TPU v7x, 32 devices: a whole 2x2x4 slice. The times are simulated.
32 devices in a mesh: dp: 8 (over z, x), seq: 4 (over y, core).
Axes of the slice: x: 2, y: 2, z: 4, core: 2. Of those that a mesh axis runs over, the one named last changes fastest.
Arguments:
- tokens: bfloat16 [96, 512, 768], P('dp', 'seq'), may hold values from -6 to 6
- lengths: int32 [96], P('dp'), may hold values from 20 to 512, as said below
- cotangent: bfloat16 [96, 512, 768], P('dp', 'seq'), may hold values from -6 to 6
- w_query: bfloat16 [768, 768], replicated, may hold values from -0.21875 to 0.21875
- w_key: bfloat16 [768, 768], replicated, may hold values from -0.21875 to 0.21875
- w_value: bfloat16 [768, 768], replicated, may hold values from -0.21875 to 0.21875
- w_out: bfloat16 [768, 768], replicated, may hold values from -0.875 to 0.875
- w_inner: bfloat16 [768, 3072], replicated, may hold values from -0.21875 to 0.21875
- w_outer: bfloat16 [3072, 768], replicated, may hold values from -0.109375 to 0.109375
- down_one: bfloat16 [768, 64], replicated, may hold values from -0.21875 to 0.21875
- up_one: bfloat16 [64, 768], replicated, may hold values from -0.75 to 0.75
- down_two: bfloat16 [768, 64], replicated, may hold values from -0.21875 to 0.21875
- up_two: bfloat16 [64, 768], replicated, may hold values from -0.75 to 0.75
- gain_one: float32 [768], replicated, may hold values from 0.5 to 1.5
- bias_one: float32 [768], replicated, may hold values from -3 to 3
- gain_two: float32 [768], replicated, may hold values from 0.5 to 1.5
- bias_two: float32 [768], replicated, may hold values from -3 to 3
Outputs:
- output: bfloat16 [96, 512, 768], P('dp', 'seq')
- input_grad: float32 [96, 512, 768], P('dp', 'seq')
- grad_down_one: float32 [768, 64], replicated
- grad_up_one: float32 [64, 768], replicated
- grad_down_two: float32 [768, 64], replicated
- grad_up_two: float32 [64, 768], replicated
- grad_gain_one: float32 [768], replicated
- grad_bias_one: float32 [768], replicated
- grad_gain_two: float32 [768], replicated
- grad_bias_two: float32 [768], replicated
Inputs may be any that keep to these rules, and one draw needn't show every extreme that they name: `lengths`: among the 12 sequences of each index of dp, one has exactly 512 tokens and another exactly 20.
All inputs are finite; a program needn't handle non-finite values.
Results may differ from a plain program's by a relative error of at most 0.015.
Values may be sent and summed in bfloat16 or wider, within the bound.
A program may use at most 320 MiB of HBM per device.

v0:
```python
import jax
import jax.numpy as jnp
from jax import lax
from jax.sharding import PartitionSpec as P

HEADS = 12
EPS = 1e-06


def matmul(left, right):
    return jnp.dot(left, right, preferred_element_type=jnp.float32)


def matmul_rt(left, right):
    return lax.dot_general(
        left, right, (((1,), (1,)), ((), ())), preferred_element_type=jnp.float32
    )


def matmul_lt(left, right):
    return lax.dot_general(
        left, right, (((0,), (0,)), ((), ())), preferred_element_type=jnp.float32
    )


def gelu_slope(value):
    return (
        0.5 * (1.0 + lax.erf(value * 0.7071067811865476))
        + value * jnp.exp(-0.5 * value * value) * 0.3989422804014327
    )


def norm_forward(hidden, gain, bias):
    mean = jnp.mean(hidden, axis=-1, keepdims=True)
    centred = hidden - mean
    inverse = lax.rsqrt(jnp.mean(centred * centred, axis=-1, keepdims=True) + EPS)
    normed = centred * inverse
    return (normed * gain + bias, normed, inverse)


def norm_backward(grad, normed, inverse, gain):
    scaled = grad * gain
    inner = (
        scaled
        - jnp.mean(scaled, axis=-1, keepdims=True)
        - normed * jnp.mean(scaled * normed, axis=-1, keepdims=True)
    )
    return (inner * inverse, jnp.sum(grad * normed, axis=0), jnp.sum(grad, axis=0))


def split_pair(values):
    upper = values.astype(jnp.bfloat16)
    lower = (values - upper.astype(jnp.float32)).astype(jnp.bfloat16)
    return (upper, lower)


def attend_forward(block):
    query, key, value, valid = block
    scale = query.shape[-1] ** (-0.5)
    scores = jnp.einsum("gqhd,gnkhd->ghqnk", query, key, preferred_element_type=jnp.float32) * scale
    mask = valid[:, None, None, :, :]
    masked = jnp.where(mask, scores, -1e30)
    top = jnp.max(masked, axis=4, keepdims=True)
    expo = jnp.where(mask, jnp.exp(masked - top), 0.0)
    total = jnp.sum(expo, axis=4, keepdims=True)
    peak = jnp.max(top, axis=3, keepdims=True)
    weight = jnp.exp(top - peak)
    denom = jnp.sum(total * weight, axis=3)
    part = jnp.einsum(
        "ghqnk,gnkhd->ghqnd", expo.astype(jnp.bfloat16), value, preferred_element_type=jnp.float32
    )
    attn = jnp.sum(part * weight, axis=3) / denom
    lse = peak[:, :, :, :, 0] + jnp.log(denom)
    return (attn.transpose(0, 2, 1, 3), top, lse)


def attend_backward(block):
    query, key, value, valid, top, lse, grad_ctx, attn = block
    scale = query.shape[-1] ** (-0.5)
    scores = jnp.einsum("gqhd,gnkhd->ghqnk", query, key, preferred_element_type=jnp.float32) * scale
    mask = valid[:, None, None, :, :]
    expo = jnp.where(mask, jnp.exp(jnp.where(mask, scores, -1e30) - top), 0.0)
    prob = jnp.where(mask, jnp.exp(scores - lse[..., None]), 0.0)
    grad_prob = jnp.einsum("gqhd,gnkhd->ghqnk", grad_ctx, value, preferred_element_type=jnp.float32)
    grad_wide = grad_ctx.astype(jnp.float32)
    delta = jnp.sum(grad_wide * attn, axis=3).transpose(0, 2, 1)[..., None, None]
    grad_scores = (prob * (grad_prob - delta)).astype(jnp.bfloat16)
    grad_query = (
        jnp.einsum("ghqnk,gnkhd->gqhd", grad_scores, key, preferred_element_type=jnp.float32)
        * scale
    )
    grad_key = (
        jnp.einsum("ghqnk,gqhd->gnkhd", grad_scores, query, preferred_element_type=jnp.float32)
        * scale
    )
    factor = jnp.exp(top - lse[..., None]).transpose(0, 3, 2, 1, 4)
    weighted = grad_wide[:, None, :, :, :] * factor
    upper, lower = split_pair(weighted)
    expo_low = expo.astype(jnp.bfloat16)
    grad_value = jnp.einsum(
        "ghqnk,gnqhd->gnkhd", expo_low, upper, preferred_element_type=jnp.float32
    )
    grad_value = grad_value + jnp.einsum(
        "ghqnk,gnqhd->gnkhd", expo_low, lower, preferred_element_type=jnp.float32
    )
    return (grad_query, grad_key, grad_value)


def per_device(
    tokens,
    lengths,
    cotangent,
    w_query,
    w_key,
    w_value,
    w_out,
    w_inner,
    w_outer,
    down_one,
    up_one,
    down_two,
    up_two,
    gain_one,
    bias_one,
    gain_two,
    bias_two,
):
    batch, rows, width = tokens.shape
    parts = lax.axis_size("seq")
    heads = HEADS
    head = width // heads
    count = batch * rows
    whole = parts * rows
    span = max(1, min(batch, 512 // rows))
    blocks = batch // span
    flat = tokens.reshape(count, width)
    query = matmul(flat, w_query).astype(jnp.bfloat16)
    key_own = matmul(flat, w_key).astype(jnp.bfloat16).reshape(batch, rows, width)
    value_own = matmul(flat, w_value).astype(jnp.bfloat16).reshape(batch, rows, width)
    key_all, value_all = (
        lax.all_gather(key_own, "seq", axis=1, tiled=True),
        lax.all_gather(value_own, "seq", axis=1, tiled=True),
    )
    valid = jnp.arange(whole).reshape(1, parts, rows) < lengths.reshape(batch, 1, 1)
    query_blocks = query.reshape(blocks, span, rows, heads, head)
    key_blocks = key_all.reshape(blocks, span, parts, rows, heads, head)
    value_blocks = value_all.reshape(blocks, span, parts, rows, heads, head)
    valid_blocks = valid.reshape(blocks, span, parts, rows)
    attn, top, lse = lax.map(attend_forward, (query_blocks, key_blocks, value_blocks, valid_blocks))
    ctx = attn.reshape(count, width).astype(jnp.bfloat16)
    out_proj = matmul(ctx, w_out)
    out_low = out_proj.astype(jnp.bfloat16)
    zed_one = matmul(out_low, down_one)
    gelu_one = jax.nn.gelu(zed_one, approximate=False).astype(jnp.bfloat16)
    branch_one = matmul(gelu_one, up_one)
    hidden_one = flat.astype(jnp.float32) + out_proj + branch_one
    normed_one, unit_one, inverse_one = norm_forward(hidden_one, gain_one, bias_one)
    normed_low = normed_one.astype(jnp.bfloat16)
    inner = matmul(normed_low, w_inner)
    hidden_low = jax.nn.gelu(inner, approximate=False).astype(jnp.bfloat16)
    ffn_out = matmul(hidden_low, w_outer)
    ffn_low = ffn_out.astype(jnp.bfloat16)
    zed_two = matmul(ffn_low, down_two)
    gelu_two = jax.nn.gelu(zed_two, approximate=False).astype(jnp.bfloat16)
    branch_two = matmul(gelu_two, up_two)
    hidden_two = normed_one + ffn_out + branch_two
    result, unit_two, inverse_two = norm_forward(hidden_two, gain_two, bias_two)
    output = result.astype(jnp.bfloat16).reshape(batch, rows, width)
    grad_out = cotangent.reshape(count, width).astype(jnp.float32)
    grad_two, grad_gain_two, grad_bias_two = norm_backward(
        grad_out, unit_two, inverse_two, gain_two
    )
    grad_branch_two = grad_two.astype(jnp.bfloat16)
    grad_up_two = matmul_lt(gelu_two, grad_branch_two)
    grad_zed_two = (matmul_rt(grad_branch_two, up_two) * gelu_slope(zed_two)).astype(jnp.bfloat16)
    grad_down_two = matmul_lt(ffn_low, grad_zed_two)
    grad_ffn = (grad_two + matmul_rt(grad_zed_two, down_two)).astype(jnp.bfloat16)
    grad_inner = (matmul_rt(grad_ffn, w_outer) * gelu_slope(inner)).astype(jnp.bfloat16)
    grad_normed = grad_two + matmul_rt(grad_inner, w_inner)
    grad_one, grad_gain_one, grad_bias_one = norm_backward(
        grad_normed, unit_one, inverse_one, gain_one
    )
    grad_branch_one = grad_one.astype(jnp.bfloat16)
    grad_up_one = matmul_lt(gelu_one, grad_branch_one)
    grad_zed_one = (matmul_rt(grad_branch_one, up_one) * gelu_slope(zed_one)).astype(jnp.bfloat16)
    grad_down_one = matmul_lt(out_low, grad_zed_one)
    grad_proj = (grad_one + matmul_rt(grad_zed_one, down_one)).astype(jnp.bfloat16)
    grad_ctx = matmul_rt(grad_proj, w_out).astype(jnp.bfloat16)
    grad_ctx_blocks = grad_ctx.reshape(blocks, span, rows, heads, head)
    grad_query, grad_key, grad_value = lax.map(
        attend_backward,
        (query_blocks, key_blocks, value_blocks, valid_blocks, top, lse, grad_ctx_blocks, attn),
    )
    key_terms = grad_key.reshape(batch, whole, width)
    value_terms = grad_value.reshape(batch, whole, width)
    key_sum, value_sum = (
        lax.psum_scatter(
            key_terms.astype(jnp.bfloat16), "seq", scatter_dimension=1, tiled=True
        ).astype(jnp.float32),
        lax.psum_scatter(
            value_terms.astype(jnp.bfloat16), "seq", scatter_dimension=1, tiled=True
        ).astype(jnp.float32),
    )
    grad_query = grad_query.reshape(count, width).astype(jnp.bfloat16)
    grad_key_low = key_sum.reshape(count, width).astype(jnp.bfloat16)
    grad_value_low = value_sum.reshape(count, width).astype(jnp.bfloat16)
    grad_input = (
        grad_one
        + matmul_rt(grad_query, w_query)
        + matmul_rt(grad_key_low, w_key)
        + matmul_rt(grad_value_low, w_value)
    )
    sums = lax.psum(
        (
            grad_down_one,
            grad_up_one,
            grad_down_two,
            grad_up_two,
            grad_gain_one,
            grad_bias_one,
            grad_gain_two,
            grad_bias_two,
        ),
        ("dp", "seq"),
    )
    return (
        output,
        grad_input.reshape(batch, rows, width),
        sums[0],
        sums[1],
        sums[2],
        sums[3],
        sums[4],
        sums[5],
        sums[6],
        sums[7],
    )


def solution(mesh):
    placed = (
        P("dp", "seq", None),
        P("dp"),
        P("dp", "seq", None),
        P(),
        P(),
        P(),
        P(),
        P(),
        P(),
        P(),
        P(),
        P(),
        P(),
        P(),
        P(),
        P(),
        P(),
    )
    return jax.shard_map(
        per_device,
        mesh=mesh,
        in_specs=placed,
        out_specs=(
            P("dp", "seq", None),
            P("dp", "seq", None),
            P(),
            P(),
            P(),
            P(),
            P(),
            P(),
            P(),
            P(),
        ),
        check_vma=False,
    )
```

profile of v0, /device:TPU:0, one launch (start us, length us, event | category | flops | bytes accessed | tf_op | source)
XLA Modules:
  0.0 864.3 jit_solution(5557883260030518720)
XLA Ops:
  7.2 4.1 convolution_convert_fusion.1
  13.8 4.0 convolution_convert_fusion.3
  20.5 5.5 convolution_convert_fusion.2
  26.0 3.4 copy.90
  38.3 43.8 %all-gather.5.cloned.1.call-done = bf16[12,512,768]{1,2,0:T(8,128)(2,1)} async-done(((bf16[12,128,768]{1,2,0:T(8,128)(2,1)}), bf16[12,512,768]{1,2,0:T(8,128)(2,1)}) %all-gather.5.cloned.1.call-update) | async-done | bytes 9437200 | tf_op jit(solution)/shard_map/all_gather | solution.py:141
  82.1 14.3 %reshape.218 = bf16[3,4,4,128,12,64]{3,2,5,4,1,0:T(4,128)(2,1)} reshape(bf16[12,512,768]{1,2,0:T(8,128)(2,1)} %all-gather.5.cloned.1.call-done) | data formatting | bytes 18874368 | tf_op jit(solution)/shard_map/reshape | solution.py:146
  96.5 10.5 %copy.94 = bf16[3,4,4,128,12,64]{3,5,2,4,1,0:T(8,128)(2,1)} copy(bf16[3,4,4,128,12,64]{3,2,5,4,1,0:T(4,128)(2,1)} %reshape.218) | data formatting | bytes 18874368 | tf_op jit(solution)/shard_map/while | solution.py:149
  107.0 42.9 %all-gather.3.cloned.1.call-done = bf16[12,512,768]{1,2,0:T(8,128)(2,1)} async-done(((bf16[12,128,768]{1,2,0:T(8,128)(2,1)}), bf16[12,512,768]{1,2,0:T(8,128)(2,1)}) %all-gather.3.cloned.1.call-update) | async-done | bytes 9437200 | tf_op jit(solution)/shard_map/all_gather | solution.py:142
  149.8 13.9 %reshape.212 = bf16[3,4,4,128,12,64]{3,2,5,4,1,0:T(4,128)(2,1)} reshape(bf16[12,512,768]{1,2,0:T(8,128)(2,1)} %all-gather.3.cloned.1.call-done) | data formatting | bytes 18874368 | tf_op jit(solution)/shard_map/reshape | solution.py:147
  163.7 10.3 %copy.92 = bf16[3,4,4,128,12,64]{3,5,2,4,1,0:T(8,128)(2,1)} copy(bf16[3,4,4,128,12,64]{3,2,5,4,1,0:T(4,128)(2,1)} %reshape.212) | data formatting | bytes 18874368 | tf_op jit(solution)/shard_map/while | solution.py:149
  174.0 68.2 %while.30 = (s32[]{:T(128)}, f32[3,4,128,12,64]{2,4,3,1,0:T(8,128)}, f32[3,4,12,128,4,1]{3,4,2,1,5,0:T(4,128)}, f32[3,4,12,128,1]{3,2,1,4,0:T(8,128)}, bf16[3,4,...) while((s32[]{:T(128)}, ...), condition=%wide.region_6.7_spmd.clone, body=%wide.region_0.6_spmd.sunk.clone | while | flops 852510720 | bytes 50842764 | solution.py:149
  174.0 4.8 fusion.260
  178.9 4.5 fusion.261
  184.7 7.1 fusion.262
  196.7 4.8 fusion.260
  201.5 4.5 fusion.261
  207.3 7.1 fusion.262
  219.4 4.8 fusion.260
  224.2 4.5 fusion.261
  230.0 7.1 fusion.262
  242.2 3.8 convert_element_type.130
  246.0 3.2 copy.95
  249.2 5.0 convert_element_type.131
  254.3 3.9 fusion.187
  264.4 11.0 %fusion.96 = f32[1536,3072]{1,0:T(8,128)} fusion(bf16[768,3072]{1,0:T(8,128)(2,1)S(1)} %bitcast.307, f32[1536,768]{1,0:T(8,128)S(1)} %get-tuple-element.271, f32[768]{0:T(1024)S(1)} %copy-done.45, f32[768]{0:T(1024)S(1)} %copy-done.41, f32[1536]{0:T(1024)S(1)} %add_rsqrt_fusion.1, f32[1536]{0:T(1024)S(1)} %broadcast_multiply_fusion.4), kind=kOutput, calls=%fused_computation.143 | convolution fusion | flops 7253655552 | bytes 28329984 | tf_op jit(solution)/shard_map/dot_general | solution.py:11
  275.4 49.7 %fusion.85 = f32[1536,768]{1,0:T(8,128)S(1)} fusion(bf16[3072,768]{1,0:T(8,128)(2,1)S(1)} %bitcast.305, f32[1536,3072]{1,0:T(8,128)} %fusion.96), kind=kOutput, calls=%fused_computation.110 | convolution fusion | flops 7554465792 | bytes 28311552 | tf_op jit(solution)/shard_map/dot_general | solution.py:11
  334.2 3.4 fusion.90
  341.2 25.4 %multiply_reduce_fusion.1 = (f32[768]{0:T(1024)}, f32[1536]{0:T(1024)}, f32[1536]{0:T(1024)}, f32[768]{0:T(1024)}, f32[1536,768]{1,0:T(8,128)}) fusion(f32[1536,768]{1,0:T(8,128)} %copy-done.10, f32[1536]{0:T(1024)S(1)} %add_rsqrt_fusion.1, f32[1536]{0:T(1024)S(1)} %broadcast_multiply_fusion.4, f32[768]{0:T(1024)} %param.34, f32[1536,768]{1,0:T(8,128)} %copy-done.4, ...), kind=kOutput, calls=%fused_computation.122 | convolution fusion | flops 14554491904 | bytes 44860416 | tf_op jit(solution)/shard_map/dot_general | solution.py:15
  367.3 4.7 subtract_multiply_fusion
  375.7 6.4 convolution_convert_fusion
  382.0 4.5 copy.96
  386.5 5.2 reshape.220
  391.7 106.8 %while.31 = (s32[]{:T(128)}, bf16[3,4,128,12,64]{2,4,3,1,0:T(8,128)(2,1)}, bf16[3,4,4,128,12,64]{3,5,2,4,1,0:T(8,128)(2,1)}, bf16[3,4,4,128,12,64]{3,5,4,2,1,0:T...) while((s32[]{:T(128)}, ...), condition=%wide.region_17.18_spmd.clone, body=%wide.region_15.17_spmd.sunk.clone | while | flops 2466662400 | bytes 130804952 | solution.py:190
  398.8 8.7 %select_convert_fusion.3 = (bf16[4,12,128,4,128]{4,2,3,1,0:T(8,128)(2,1)S(1)}, f32[4,12,128,4,128]{4,2,3,1,0:T(8,128)}) fusion(f32[4,12,128,4]{2,3,1,0:T(4,128)S(1)} %dynamic-slice_bitcast_fusion.13, pred[4,4,128]{2,1,0:T(4,128)(4,1)S(1)} %dynamic-slice_bitcast_fusion.14, bf16[3,4,4,128,12,64]{3,5,2,4,1,0:T(8,128)(2,1)} %get-tuple-element.519, ...), kind=kOutput, calls=%fused_computation.33.clone.1.clone | convolution fusion | flops 418381824 | bytes 22907904 | tf_op jit(solution)/shard_map/while/body/eval_jaxpr/gqhd,gnkhd->ghqnk/dot_general | solution.py:80
  407.4 8.1 multiply_convert_fusion.10
  415.6 4.3 bitcast_dynamic-update-slice_fusion.21
  424.4 3.2 bitcast_dynamic-update-slice_fusion.23
  434.2 8.7 %select_convert_fusion.3 = (bf16[4,12,128,4,128]{4,2,3,1,0:T(8,128)(2,1)S(1)}, f32[4,12,128,4,128]{4,2,3,1,0:T(8,128)}) fusion(f32[4,12,128,4]{2,3,1,0:T(4,128)S(1)} %dynamic-slice_bitcast_fusion.13, pred[4,4,128]{2,1,0:T(4,128)(4,1)S(1)} %dynamic-slice_bitcast_fusion.14, bf16[3,4,4,128,12,64]{3,5,2,4,1,0:T(8,128)(2,1)} %get-tuple-element.519, ...), kind=kOutput, calls=%fused_computation.33.clone.1.clone | convolution fusion | flops 418381824 | bytes 22907904 | tf_op jit(solution)/shard_map/while/body/eval_jaxpr/gqhd,gnkhd->ghqnk/dot_general | solution.py:80
  442.9 8.1 multiply_convert_fusion.10
  451.0 4.3 bitcast_dynamic-update-slice_fusion.21
  459.8 3.2 bitcast_dynamic-update-slice_fusion.23
  469.6 8.7 %select_convert_fusion.3 = (bf16[4,12,128,4,128]{4,2,3,1,0:T(8,128)(2,1)S(1)}, f32[4,12,128,4,128]{4,2,3,1,0:T(8,128)}) fusion(f32[4,12,128,4]{2,3,1,0:T(4,128)S(1)} %dynamic-slice_bitcast_fusion.13, pred[4,4,128]{2,1,0:T(4,128)(4,1)S(1)} %dynamic-slice_bitcast_fusion.14, bf16[3,4,4,128,12,64]{3,5,2,4,1,0:T(8,128)(2,1)} %get-tuple-element.519, ...), kind=kOutput, calls=%fused_computation.33.clone.1.clone | convolution fusion | flops 418381824 | bytes 22907904 | tf_op jit(solution)/shard_map/while/body/eval_jaxpr/gqhd,gnkhd->ghqnk/dot_general | solution.py:80
  478.3 8.1 multiply_convert_fusion.10
  486.5 4.3 bitcast_dynamic-update-slice_fusion.21
  495.4 3.2 bitcast_dynamic-update-slice_fusion.23
  498.5 12.3 %copy.105 = bf16[3,4,4,128,12,64]{3,2,5,4,1,0:T(4,128)(2,1)} copy(bf16[3,4,4,128,12,64]{3,5,4,2,1,0:T(8,128)(2,1)} %get-tuple-element.123) | data formatting | bytes 18874368 | tf_op jit(solution)/shard_map/convert_element_type | solution.py:201
  510.8 14.6 %convert_element_type.156 = bf16[12,512,768]{1,2,0:T(8,128)(2,1)} reshape(bf16[3,4,4,128,12,64]{3,2,5,4,1,0:T(4,128)(2,1)} %copy.105) | data formatting | bytes 18874368 | tf_op jit(solution)/shard_map/convert_element_type | solution.py:201
  525.4 16.4 %copy.114 = bf16[12,512,768]{2,0,1:T(8,128)(2,1)} copy(bf16[12,512,768]{1,2,0:T(8,128)(2,1)} %convert_element_type.156) | data formatting | bytes 18874368
  541.8 13.1 %copy.132 = bf16[64,8,12,768]{3,1,2,0:T(8,128)(2,1)} copy(bf16[64,8,12,768]{3,2,1,0:T(8,128)(2,1)} %bitcast.282) | data formatting | bytes 18874368
  555.0 12.3 %copy.103 = bf16[3,4,4,128,12,64]{3,2,5,4,1,0:T(4,128)(2,1)} copy(bf16[3,4,4,128,12,64]{3,5,2,4,1,0:T(8,128)(2,1)} %get-tuple-element.122) | data formatting | bytes 18874368 | tf_op jit(solution)/shard_map/convert_element_type | solution.py:198
  567.3 15.1 %convert_element_type.153 = bf16[12,512,768]{1,2,0:T(8,128)(2,1)} reshape(bf16[3,4,4,128,12,64]{3,2,5,4,1,0:T(4,128)(2,1)} %copy.103) | data formatting | bytes 18874368 | tf_op jit(solution)/shard_map/convert_element_type | solution.py:198
  582.4 16.3 %copy.112 = bf16[12,512,768]{2,0,1:T(8,128)(2,1)} copy(bf16[12,512,768]{1,2,0:T(8,128)(2,1)} %convert_element_type.153) | data formatting | bytes 18874368
  598.7 13.4 %copy.131 = bf16[64,8,12,768]{3,1,2,0:T(8,128)(2,1)} copy(bf16[64,8,12,768]{3,2,1,0:T(8,128)(2,1)} %bitcast.283) | data formatting | bytes 18874368
  613.8 3.2 copy.102
  617.0 5.1 convert_element_type.151
  622.1 40.2 %all-reduce = (f32[768]{0:T(1024)}, f32[768]{0:T(1024)}, f32[768]{0:T(1024)}, f32[768]{0:T(1024)}) all-reduce(f32[768]{0:T(1024)S(1)} %copy-done.39, f32[768]{0:T(1024)S(1)} %copy-done.40, f32[768]{0:T(1024)S(1)} %copy-done.36, f32[768]{0:T(1024)S(1)} %copy-done.37), channel_id=1, replica_groups=mesh['dp'=8,'seq'=4] {'dp','seq'}, use_global_device_ids=true, to_apply=%region_25.26 | all-reduce | flops 3072 | bytes 24576 | tf_op jit(solution)/shard_map/psum | solution.py:213
  662.3 3.7 fusion.110
  666.1 3.7 fusion.114
  673.6 5.5 fusion.188
  679.2 4.8 reshape.230
  686.6 28.4 %reduce-scatter.7.cloned.1.call-done = bf16[128,9216]{1,0:T(8,128)(2,1)} async-done(((bf16[512,9216]{1,0:T(8,128)(2,1)}), bf16[128,9216]{1,0:T(8,128)(2,1)}) %reduce-scatter.7.cloned.1.call-update) | async-done | bytes 2359312
  715.0 5.0 reshape.228
  725.2 4.7 add_add_fusion
  729.9 121.2 %all-reduce.4.cloned.1.call-done = (f32[768,64]{0,1:T(8,128)}, f32[64,768]{1,0:T(8,128)}, f32[768,64]{0,1:T(8,128)}, f32[64,768]{1,0:T(8,128)}) async-done(((f32[768,64]{0,1:T(8,128)}, f32[64,768]{1,0:T(8,128)}, f32[768,64]{0,1:T(8,128)}, f32[64,768]{1,0:T(8,128)}), (f32[768,64]{0,1:T(8,128)}, f32[64,768]{1,0:T(8,128)}, f32[768,64]{0,1:T(8,128)}, f32[64,768]{1,0:T(8,128)})) %all-reduce.4.cloned.1.call-update) | async-done | bytes 786448 | tf_op jit(solution)/shard_map/psum | solution.py:213
  (230 shorter events, 108.9 us)
Async XLA Ops:
  7.2 247.1 %copy-start = (bf16[768,768]{1,0:T(8,128)(2,1)S(1)}, bf16[768,768]{1,0:T(8,128)(2,1)}, u32[]{:S(2)}) copy-start(bf16[768,768]{1,0:T(8,128)(2,1)} %param.27) | copy-start | bytes 3538948
  7.2 75.0 %all-gather.5.cloned.1.call-start = ((), (), s32[]{:S(2)}) async-start(), calls=%async_computation.3 | async-start | bytes 11796480 | tf_op jit(solution)/shard_map/all_gather | solution.py:141
  13.8 136.0 %all-gather.3.cloned.1.call-start = ((), (), s32[]{:S(2)}) async-start(), calls=%async_computation.2 | async-start | bytes 11796480 | tf_op jit(solution)/shard_map/all_gather | solution.py:142
  17.8 2.6 copy-start.42
  20.3 658.9 %reduce-scatter.9.cloned.1.call-start = ((), (), s32[]{:S(2)}) async-start(), calls=%async_computation.5 | async-start | bytes 11796480
  31.5 4.6 copy-start.6
  31.5 4.6 copy-start.33
  183.3 1.3 copy-start.14
  242.2 7.0 copy-start.2
  242.2 7.0 copy-start.27
  254.3 3.9 copy-start.31
  254.3 4.8 copy-start.43
  258.2 2.9 copy-start.8
  258.2 4.5 slice-start.10
  259.2 1.9 copy-start.18
  259.2 4.1 slice-start.11
  259.2 16.2 %slice-start.8 = ((s8[4718592]{0:T(1024)(128)(4,1)}), s8[4194304]{0:T(1024)(128)(4,1)S(1)}, s32[]{:S(2)}) async-start(s8[4718592]{0:T(1024)(128)(4,1)} %bitcast.304), calls=%async_computation.15 | async-start | bytes 8388608
  261.2 64.8 %copy-start.10 = (f32[1536,768]{1,0:T(8,128)}, f32[1536,768]{1,0:T(8,128)S(1)}, u32[]{:S(2)}) copy-start(f32[1536,768]{1,0:T(8,128)S(1)} %get-tuple-element.271) | copy-start | bytes 14155780
  261.2 3.2 copy-start.41
  261.2 3.2 copy-start.45
  264.4 11.0 %slice-start.9 = ((s8[4718592]{0:T(1024)(128)(4,1)}), s8[524288]{0:T(1024)(128)(4,1)S(1)}, s32[]{:S(2)}) async-start(s8[4718592]{0:T(1024)(128)(4,1)} %bitcast.304), calls=%async_computation.16 | async-start | bytes 1048576
  275.4 49.7 %copy-start.26 = (bf16[768,64]{0,1:T(8,128)(2,1)S(1)}, bf16[768,64]{0,1:T(8,128)(2,1)}, u32[]{:S(2)}) copy-start(bf16[768,64]{0,1:T(8,128)(2,1)} %param.32) | copy-start | bytes 294916
  325.1 2.1 copy-start.9
  325.1 2.1 copy-start.28
  327.3 10.3 %copy-start.21 = (f32[1536,64]{0,1:T(8,128)}, f32[1536,64]{0,1:T(8,128)S(1)}, u32[]{:S(2)}) copy-start(f32[1536,64]{0,1:T(8,128)S(1)} %fusion.112) | copy-start | bytes 1179652
  329.8 1.7 copy-start.7
  329.8 1.7 copy-start.34
  330.5 3.7 copy-start.35
  330.5 3.7 copy-start.38
  337.6 2.1 copy-start.4
  367.3 6.8 copy-start.19
  367.3 6.8 copy-start.30
  372.0 2.1 copy-start.5
  374.1 1.5 copy-start.32
  382.0 9.7 %copy-start.3 = (bf16[3,4,128,12,64]{2,4,3,1,0:T(8,128)(2,1)S(1)}, bf16[3,4,128,12,64]{2,4,3,1,0:T(8,128)(2,1)}, u32[]{:S(2)}) copy-start(bf16[3,4,128,12,64]{2,4,3,1,0:T(8,128)(2,1)} %copy-done.2) | copy-start | bytes 7077892
  407.4 8.1 copy-start.11
  419.9 2.6 copy-start.12
  442.9 8.1 copy-start.11
  455.4 2.7 copy-start.12
  478.3 8.1 copy-start.11
  490.8 2.8 copy-start.12
  555.0 160.0 %reduce-scatter.7.cloned.1.call-start = ((), (), s32[]{:S(2)}) async-start(), calls=%async_computation.4 | async-start | bytes 11796480
  612.1 1.7 copy-start.13
  612.1 238.9 %all-reduce.4.cloned.1.call-start = ((), (), s32[]{:S(2)}) async-start(), calls=%async_computation.6 | async-start | bytes 1572864 | tf_op jit(solution)/shard_map/psum | solution.py:213
  613.8 8.3 copy-start.36
  613.8 8.3 copy-start.37
  613.8 8.3 copy-start.39
  613.8 8.3 copy-start.40
  613.8 48.6 %copy-start.17 = (bf16[1536,64]{0,1:T(8,128)(2,1)S(1)}, bf16[1536,64]{0,1:T(8,128)(2,1)}, u32[]{:S(2)}) copy-start(bf16[1536,64]{0,1:T(8,128)(2,1)} %copy-done.16) | copy-start | bytes 589828
  617.0 49.0 %copy-start.25 = (bf16[1536,64]{0,1:T(8,128)(2,1)S(1)}, bf16[1536,64]{0,1:T(8,128)(2,1)}, u32[]{:S(2)}) copy-start(bf16[1536,64]{0,1:T(8,128)(2,1)} %copy-done.24) | copy-start | bytes 589828
  622.1 47.6 %slice-start = ((s8[4718592]{0:T(1024)(128)(4,1)}), s8[524288]{0:T(1024)(128)(4,1)S(1)}, s32[]{:S(2)}) async-start(s8[4718592]{0:T(1024)(128)(4,1)} %bitcast.284), calls=%async_computation.7 | async-start | bytes 1048576
  662.3 7.4 slice-start.1
  662.3 7.4 copy-start.22
  666.1 5.6 slice-start.2
  669.8 1.9 slice-start.3
  669.8 1.9 copy-start.20
  671.7 1.9 copy-start.15
  686.6 36.2 %copy-start.44 = (bf16[768,768]{1,0:T(8,128)(2,1)S(1)}, bf16[768,768]{1,0:T(8,128)(2,1)}, u32[]{:S(2)}) copy-start(bf16[768,768]{1,0:T(8,128)(2,1)} %param.25) | copy-start | bytes 3538948
  720.0 4.9 slice-start.4
  720.0 4.9 slice-start.6
  722.8 2.1 slice-start.5
  722.8 2.1 slice-start.7
  722.8 2.4 copy-start.23
  725.2 132.3 %copy-start.1 = (bf16[768,768]{1,0:T(8,128)(2,1)S(1)}, bf16[768,768]{1,0:T(8,128)(2,1)}, u32[]{:S(2)}) copy-start(bf16[768,768]{1,0:T(8,128)(2,1)} %param.27) | copy-start | bytes 3538948
  (5 other events, 5.0 us)
Sparse Core Ops, SparseCore 0:
  13.9 68.1 all-gather.4
  84.3 65.4 all-gather.2
  555.1 78.9 reduce-scatter.8
  636.5 78.4 reduce-scatter.6
  721.1 129.9 all-reduce.3
where the time goes:
time: 874 us; the launch traced here: 864 us
  matrix products  264 us (30%)
  local copies, waits for them, and re-layouts  248 us (28%)
  waiting for transfers between devices  236 us (27%)
  other arithmetic  59.3 us (7%)
  blocking collectives  40.2 us (5%)
  between operations  14.7 us (2%)
    psum x1, waiting for transfers between devices, per_device(): lax.psum((grad_down_one, grad_up_one, grad_down_two, grad_up_two, grad_ga...  121 us
    unnamed x120, local copies, waits for them, and re-layouts  87.1 us
    dot_general x10, matrix products, matmul(): return jnp.dot(left, right, preferred_element_type=jnp.float32)  84.2 us
    dot_general x8, matrix products, matmul_rt(): lax.dot_general(left, right, (((1,), (1,)), ((), ())), preferred_element_...  46.6 us
    all_gather x1, waiting for transfers between devices, per_device(): lax.all_gather(key_own, 'seq', axis=1, tiled=True)  43.8 us
    all_gather x1, waiting for transfers between devices, per_device(): lax.all_gather(value_own, 'seq', axis=1, tiled=True)  42.9 us
    psum x1, blocking collectives, per_device(): lax.psum((grad_down_one, grad_up_one, grad_down_two, grad_up_two, grad_ga...  40.2 us
    unnamed x7, waiting for transfers between devices  28.5 us
  transfers between devices with their start and end apart: 5, of which 4 were waited for; matrix products, arithmetic and copies ran while one was open for 18% of the time, Pallas kernels for 0%

commit v1 on v0

--- a/solution.py
+++ b/solution.py
@@ -211,17 +211,20 @@
         + matmul_rt(grad_value_low, w_value)
     )
     sums = lax.psum(
-        (
-            grad_down_one,
-            grad_up_one,
-            grad_down_two,
-            grad_up_two,
-            grad_gain_one,
-            grad_bias_one,
-            grad_gain_two,
-            grad_bias_two,
+        lax.psum(
+            (
+                grad_down_one,
+                grad_up_one,
+                grad_down_two,
+                grad_up_two,
+                grad_gain_one,
+                grad_bias_one,
+                grad_gain_two,
+                grad_bias_two,
+            ),
+            "seq",
         ),
-        ("dp", "seq"),
+        "dp",
     )
     return (
         output,

time: 874 us -> 819 us (0.937)
  waiting for transfers between devices: 236 us -> 182 us
  blocking collectives: 40.2 us -> 49.5 us
    psum x1, waiting for transfers between devices: 121 us -> 0.01 us  [per_device(): lax.psum((grad_down_one, grad_up_one, grad_down_two, grad_up_two, grad_ga...]
    psum x0 -> x1, waiting for transfers between devices: none -> 64.1 us  [per_device(): lax.psum(lax.psum((grad_down_one, grad_up_one, grad_down_two, grad_up_two...]
    psum x0 -> x1, blocking collectives: none -> 38.1 us  [per_device(): lax.psum(lax.psum((grad_down_one, grad_up_one, grad_down_two, grad_up_two...]
    psum x1, blocking collectives: 40.2 us -> 11.4 us  [per_device(): lax.psum((grad_down_one, grad_up_one, grad_down_two, grad_up_two, grad_ga...]
    unnamed x120 -> x98, local copies, waits for them, and re-layouts: 87.1 us -> 82.6 us
    unnamed x7 -> x8, waiting for transfers between devices: 28.5 us -> 31.3 us
  transfers between devices with their start and end apart: 5 -> 6, of which waited for: 4 -> 4; matrix products, arithmetic and copies ran while one was open for 18% -> 38% of each run, Pallas kernels for 0% -> 0%
where the time goes in v1:
time: 819 us; the launch traced here: 809 us
  matrix products  260 us (32%)
  local copies, waits for them, and re-layouts  243 us (30%)
  waiting for transfers between devices  182 us (22%)
  other arithmetic  59.6 us (7%)
  blocking collectives  49.5 us (6%)
  between operations  15.2 us (2%)
    dot_general x10, matrix products, matmul(): return jnp.dot(left, right, preferred_element_type=jnp.float32)  84.2 us
    unnamed x98, local copies, waits for them, and re-layouts  82.6 us
    psum x1, waiting for transfers between devices, per_device(): lax.psum(lax.psum((grad_down_one, grad_up_one, grad_down_two, grad_up_two...  64.1 us
    dot_general x8, matrix products, matmul_rt(): lax.dot_general(left, right, (((1,), (1,)), ((), ())), preferred_element_...  46.7 us
    all_gather x1, waiting for transfers between devices, per_device(): lax.all_gather(key_own, 'seq', axis=1, tiled=True)  43.7 us
    all_gather x1, waiting for transfers between devices, per_device(): lax.all_gather(value_own, 'seq', axis=1, tiled=True)  42.8 us
    psum x1, blocking collectives, per_device(): lax.psum(lax.psum((grad_down_one, grad_up_one, grad_down_two, grad_up_two...  38.1 us
    unnamed x8, waiting for transfers between devices  31.3 us
  transfers between devices with their start and end apart: 6, of which 4 were waited for; matrix products, arithmetic and copies ran while one was open for 38% of the time, Pallas kernels for 0%

profile of v1, /device:TPU:0, one launch (start us, length us, event | category | flops | bytes accessed | tf_op | source)
XLA Modules:
  0.0 809.5 jit_solution(6631994572117139990)
XLA Ops:
  7.2 4.1 convolution_convert_fusion.1
  13.8 4.0 convolution_convert_fusion.3
  20.5 5.5 convolution_convert_fusion.2
  26.0 3.4 copy.90
  38.4 43.7 %all-gather.5.cloned.1.call-done = bf16[12,512,768]{1,2,0:T(8,128)(2,1)} async-done(((bf16[12,128,768]{1,2,0:T(8,128)(2,1)}), bf16[12,512,768]{1,2,0:T(8,128)(2,1)}) %all-gather.5.cloned.1.call-update) | async-done | bytes 9437200 | tf_op jit(solution)/shard_map/all_gather | solution.py:141
  82.1 14.3 %reshape.218 = bf16[3,4,4,128,12,64]{3,2,5,4,1,0:T(4,128)(2,1)} reshape(bf16[12,512,768]{1,2,0:T(8,128)(2,1)} %all-gather.5.cloned.1.call-done) | data formatting | bytes 18874368 | tf_op jit(solution)/shard_map/reshape | solution.py:146
  96.4 10.5 %copy.94 = bf16[3,4,4,128,12,64]{3,5,2,4,1,0:T(8,128)(2,1)} copy(bf16[3,4,4,128,12,64]{3,2,5,4,1,0:T(4,128)(2,1)} %reshape.218) | data formatting | bytes 18874368 | tf_op jit(solution)/shard_map/while | solution.py:149
  107.0 42.8 %all-gather.3.cloned.1.call-done = bf16[12,512,768]{1,2,0:T(8,128)(2,1)} async-done(((bf16[12,128,768]{1,2,0:T(8,128)(2,1)}), bf16[12,512,768]{1,2,0:T(8,128)(2,1)}) %all-gather.3.cloned.1.call-update) | async-done | bytes 9437200 | tf_op jit(solution)/shard_map/all_gather | solution.py:142
  149.8 13.9 %reshape.212 = bf16[3,4,4,128,12,64]{3,2,5,4,1,0:T(4,128)(2,1)} reshape(bf16[12,512,768]{1,2,0:T(8,128)(2,1)} %all-gather.3.cloned.1.call-done) | data formatting | bytes 18874368 | tf_op jit(solution)/shard_map/reshape | solution.py:147
  163.7 10.3 %copy.92 = bf16[3,4,4,128,12,64]{3,5,2,4,1,0:T(8,128)(2,1)} copy(bf16[3,4,4,128,12,64]{3,2,5,4,1,0:T(4,128)(2,1)} %reshape.212) | data formatting | bytes 18874368 | tf_op jit(solution)/shard_map/while | solution.py:149
  174.0 68.3 %while.30 = (s32[]{:T(128)}, f32[3,4,128,12,64]{2,4,3,1,0:T(8,128)}, f32[3,4,12,128,4,1]{3,4,2,1,5,0:T(4,128)}, f32[3,4,12,128,1]{3,2,1,4,0:T(8,128)}, bf16[3,4,...) while((s32[]{:T(128)}, ...), condition=%wide.region_6.7_spmd.clone, body=%wide.region_0.6_spmd.sunk.clone | while | flops 852510720 | bytes 50842764 | solution.py:149
  174.0 4.8 fusion.260
  178.9 4.5 fusion.261
  184.6 7.1 fusion.262
  193.8 2.9 bitcast_dynamic-update-slice_fusion.18
  196.7 4.8 fusion.260
  201.5 4.5 fusion.261
  207.3 7.1 fusion.262
  219.3 4.8 fusion.260
  224.2 4.5 fusion.261
  230.0 7.1 fusion.262
  242.4 3.8 convert_element_type.130
  246.2 3.2 copy.95
  249.4 5.1 convert_element_type.131
  254.5 3.9 fusion.187
  264.6 11.1 %fusion.96 = f32[1536,3072]{1,0:T(8,128)} fusion(bf16[768,3072]{1,0:T(8,128)(2,1)S(1)} %bitcast.305, f32[1536,768]{1,0:T(8,128)S(1)} %get-tuple-element.279, f32[768]{0:T(1024)S(1)} %copy-done.36, f32[768]{0:T(1024)S(1)} %copy-done.32, f32[1536]{0:T(1024)S(1)} %add_rsqrt_fusion.1, f32[1536]{0:T(1024)S(1)} %broadcast_multiply_fusion.4), kind=kOutput, calls=%fused_computation.143 | convolution fusion | flops 7253655552 | bytes 28329984 | tf_op jit(solution)/shard_map/dot_general | solution.py:11
  275.6 49.6 %fusion.85 = f32[1536,768]{1,0:T(8,128)S(1)} fusion(bf16[3072,768]{1,0:T(8,128)(2,1)S(1)} %bitcast.303, f32[1536,3072]{1,0:T(8,128)} %fusion.96), kind=kOutput, calls=%fused_computation.110 | convolution fusion | flops 7554465792 | bytes 28311552 | tf_op jit(solution)/shard_map/dot_general | solution.py:11
  333.1 3.6 fusion.90
  341.5 25.3 %multiply_reduce_fusion.1 = (f32[768]{0:T(1024)}, f32[1536]{0:T(1024)}, f32[1536]{0:T(1024)}, f32[768]{0:T(1024)}, f32[1536,768]{1,0:T(8,128)}) fusion(f32[1536,768]{1,0:T(8,128)} %copy-done.9, f32[1536]{0:T(1024)S(1)} %add_rsqrt_fusion.1, f32[1536]{0:T(1024)S(1)} %broadcast_multiply_fusion.4, f32[768]{0:T(1024)} %param.34, f32[1536,768]{1,0:T(8,128)} %copy-done.4, ...), kind=kOutput, calls=%fused_computation.122 | convolution fusion | flops 14554491904 | bytes 44860416 | tf_op jit(solution)/shard_map/dot_general | solution.py:15
  367.6 4.7 subtract_multiply_fusion
  377.6 6.5 convolution_convert_fusion
  384.1 4.4 copy.96
  388.5 5.2 reshape.220
  393.8 106.8 %while.31 = (s32[]{:T(128)}, bf16[3,4,128,12,64]{2,4,3,1,0:T(8,128)(2,1)}, bf16[3,4,4,128,12,64]{3,5,2,4,1,0:T(8,128)(2,1)}, bf16[3,4,4,128,12,64]{3,5,4,2,1,0:T...) while((s32[]{:T(128)}, ...), condition=%wide.region_17.18_spmd.clone, body=%wide.region_15.17_spmd.sunk.clone | while | flops 2466662400 | bytes 130804952 | solution.py:190
  400.7 8.7 %select_convert_fusion.3 = (bf16[4,12,128,4,128]{4,2,3,1,0:T(8,128)(2,1)S(1)}, f32[4,12,128,4,128]{4,2,3,1,0:T(8,128)}) fusion(f32[4,12,128,4]{2,3,1,0:T(4,128)S(1)} %dynamic-slice_bitcast_fusion.13, pred[4,4,128]{2,1,0:T(4,128)(4,1)S(1)} %dynamic-slice_bitcast_fusion.14, bf16[3,4,4,128,12,64]{3,5,2,4,1,0:T(8,128)(2,1)} %get-tuple-element.527, ...), kind=kOutput, calls=%fused_computation.33.clone.1.clone | convolution fusion | flops 418381824 | bytes 22907904 | tf_op jit(solution)/shard_map/while/body/eval_jaxpr/gqhd,gnkhd->ghqnk/dot_general | solution.py:80
  409.4 8.2 %multiply_convert_fusion.10 = bf16[4,12,128,4,128]{4,2,3,1,0:T(8,128)(2,1)S(1)} fusion(f32[4,12,128,4,128]{4,2,3,1,0:T(8,128)} %get-tuple-element.460, f32[4,12,128]{2,1,0:T(8,128)S(1)} %bitcast.301, f32[4,12,128]{2,1,0:T(8,128)S(1)} %dynamic-slice_bitcast_fusion.15, pred[4,4,128]{2,1,0:T(4,128)(4,1)S(1)} %dynamic-slice_bitcast_fusion.14, ...), kind=kOutput, calls=%fused_computation.34.clone.1.clone | convolution fusion | flops 421527552 | bytes 22857732 | tf_op jit(solution)/shard_map/while/body/eval_jaxpr/gqhd,gnkhd->ghqnk/dot_general | solution.py:84
  417.6 4.4 bitcast_dynamic-update-slice_fusion.21
  426.4 3.2 bitcast_dynamic-update-slice_fusion.23
  436.2 8.7 %select_convert_fusion.3 = (bf16[4,12,128,4,128]{4,2,3,1,0:T(8,128)(2,1)S(1)}, f32[4,12,128,4,128]{4,2,3,1,0:T(8,128)}) fusion(f32[4,12,128,4]{2,3,1,0:T(4,128)S(1)} %dynamic-slice_bitcast_fusion.13, pred[4,4,128]{2,1,0:T(4,128)(4,1)S(1)} %dynamic-slice_bitcast_fusion.14, bf16[3,4,4,128,12,64]{3,5,2,4,1,0:T(8,128)(2,1)} %get-tuple-element.527, ...), kind=kOutput, calls=%fused_computation.33.clone.1.clone | convolution fusion | flops 418381824 | bytes 22907904 | tf_op jit(solution)/shard_map/while/body/eval_jaxpr/gqhd,gnkhd->ghqnk/dot_general | solution.py:80
  444.9 8.1 %multiply_convert_fusion.10 = bf16[4,12,128,4,128]{4,2,3,1,0:T(8,128)(2,1)S(1)} fusion(f32[4,12,128,4,128]{4,2,3,1,0:T(8,128)} %get-tuple-element.460, f32[4,12,128]{2,1,0:T(8,128)S(1)} %bitcast.301, f32[4,12,128]{2,1,0:T(8,128)S(1)} %dynamic-slice_bitcast_fusion.15, pred[4,4,128]{2,1,0:T(4,128)(4,1)S(1)} %dynamic-slice_bitcast_fusion.14, ...), kind=kOutput, calls=%fused_computation.34.clone.1.clone | convolution fusion | flops 421527552 | bytes 22857732 | tf_op jit(solution)/shard_map/while/body/eval_jaxpr/gqhd,gnkhd->ghqnk/dot_general | solution.py:84
  453.1 4.3 bitcast_dynamic-update-slice_fusion.21
  461.9 3.1 bitcast_dynamic-update-slice_fusion.23
  471.7 8.7 %select_convert_fusion.3 = (bf16[4,12,128,4,128]{4,2,3,1,0:T(8,128)(2,1)S(1)}, f32[4,12,128,4,128]{4,2,3,1,0:T(8,128)}) fusion(f32[4,12,128,4]{2,3,1,0:T(4,128)S(1)} %dynamic-slice_bitcast_fusion.13, pred[4,4,128]{2,1,0:T(4,128)(4,1)S(1)} %dynamic-slice_bitcast_fusion.14, bf16[3,4,4,128,12,64]{3,5,2,4,1,0:T(8,128)(2,1)} %get-tuple-element.527, ...), kind=kOutput, calls=%fused_computation.33.clone.1.clone | convolution fusion | flops 418381824 | bytes 22907904 | tf_op jit(solution)/shard_map/while/body/eval_jaxpr/gqhd,gnkhd->ghqnk/dot_general | solution.py:80
  480.4 8.1 %multiply_convert_fusion.10 = bf16[4,12,128,4,128]{4,2,3,1,0:T(8,128)(2,1)S(1)} fusion(f32[4,12,128,4,128]{4,2,3,1,0:T(8,128)} %get-tuple-element.460, f32[4,12,128]{2,1,0:T(8,128)S(1)} %bitcast.301, f32[4,12,128]{2,1,0:T(8,128)S(1)} %dynamic-slice_bitcast_fusion.15, pred[4,4,128]{2,1,0:T(4,128)(4,1)S(1)} %dynamic-slice_bitcast_fusion.14, ...), kind=kOutput, calls=%fused_computation.34.clone.1.clone | convolution fusion | flops 421527552 | bytes 22857732 | tf_op jit(solution)/shard_map/while/body/eval_jaxpr/gqhd,gnkhd->ghqnk/dot_general | solution.py:84
  488.6 4.3 bitcast_dynamic-update-slice_fusion.21
  497.5 3.1 bitcast_dynamic-update-slice_fusion.23
  500.6 12.2 %copy.105 = bf16[3,4,4,128,12,64]{3,2,5,4,1,0:T(4,128)(2,1)} copy(bf16[3,4,4,128,12,64]{3,5,4,2,1,0:T(8,128)(2,1)} %get-tuple-element.123) | data formatting | bytes 18874368 | tf_op jit(solution)/shard_map/convert_element_type | solution.py:201
  512.9 14.5 %convert_element_type.156 = bf16[12,512,768]{1,2,0:T(8,128)(2,1)} reshape(bf16[3,4,4,128,12,64]{3,2,5,4,1,0:T(4,128)(2,1)} %copy.105) | data formatting | bytes 18874368 | tf_op jit(solution)/shard_map/convert_element_type | solution.py:201
  527.4 16.5 %copy.114 = bf16[12,512,768]{2,0,1:T(8,128)(2,1)} copy(bf16[12,512,768]{1,2,0:T(8,128)(2,1)} %convert_element_type.156) | data formatting | bytes 18874368
  543.9 13.1 %copy.132 = bf16[64,8,12,768]{3,1,2,0:T(8,128)(2,1)} copy(bf16[64,8,12,768]{3,2,1,0:T(8,128)(2,1)} %bitcast.282) | data formatting | bytes 18874368
  557.1 12.2 %copy.103 = bf16[3,4,4,128,12,64]{3,2,5,4,1,0:T(4,128)(2,1)} copy(bf16[3,4,4,128,12,64]{3,5,2,4,1,0:T(8,128)(2,1)} %get-tuple-element.122) | data formatting | bytes 18874368 | tf_op jit(solution)/shard_map/convert_element_type | solution.py:198
  569.3 15.0 %convert_element_type.153 = bf16[12,512,768]{1,2,0:T(8,128)(2,1)} reshape(bf16[3,4,4,128,12,64]{3,2,5,4,1,0:T(4,128)(2,1)} %copy.103) | data formatting | bytes 18874368 | tf_op jit(solution)/shard_map/convert_element_type | solution.py:198
  584.3 16.3 %copy.112 = bf16[12,512,768]{2,0,1:T(8,128)(2,1)} copy(bf16[12,512,768]{1,2,0:T(8,128)(2,1)} %convert_element_type.153) | data formatting | bytes 18874368
  600.6 13.5 %copy.131 = bf16[64,8,12,768]{3,1,2,0:T(8,128)(2,1)} copy(bf16[64,8,12,768]{3,2,1,0:T(8,128)(2,1)} %bitcast.283) | data formatting | bytes 18874368
  615.8 3.2 copy.102
  619.0 4.0 convert_element_type.151
  623.0 11.4 %all-reduce.2 = (f32[768]{0:T(1024)S(1)}, f32[768]{0:T(1024)S(1)}, f32[768]{0:T(1024)S(1)}, f32[768]{0:T(1024)S(1)}) all-reduce(f32[768]{0:T(1024)S(1)} %copy-done.30, f32[768]{0:T(1024)S(1)} %copy-done.31, f32[768]{0:T(1024)S(1)} %copy-done.27, f32[768]{0:T(1024)S(1)} %copy-done.28), channel_id=1, replica_groups=mesh['dp'=8,'seq'=4] {'seq'}, use_global_device_ids=true, to_apply=%region_29.30 | all-reduce | flops 3072 | bytes 24576 | tf_op jit(solution)/shard_map/psum | solution.py:214
  634.4 38.1 %all-reduce = (f32[768]{0:T(1024)}, f32[768]{0:T(1024)}, f32[768]{0:T(1024)}, f32[768]{0:T(1024)}) all-reduce(f32[768]{0:T(1024)S(1)} %get-tuple-element.262, f32[768]{0:T(1024)S(1)} %get-tuple-element.263, f32[768]{0:T(1024)S(1)} %get-tuple-element.264, f32[768]{0:T(1024)S(1)} %get-tuple-element.265), channel_id=1, replica_groups=mesh['dp'=8,'seq'=4] {'dp'}, use_global_device_ids=true, to_apply=%region_30.31 | all-reduce | flops 3072 | bytes 24576 | tf_op jit(solution)/shard_map/psum | solution.py:213
  672.5 5.6 fusion.188
  678.1 4.8 reshape.230
  685.6 31.2 %reduce-scatter.7.cloned.1.call-done = bf16[128,9216]{1,0:T(8,128)(2,1)} async-done(((bf16[512,9216]{1,0:T(8,128)(2,1)}), bf16[128,9216]{1,0:T(8,128)(2,1)}) %reduce-scatter.7.cloned.1.call-update) | async-done | bytes 2359312
  716.8 4.8 reshape.228
  727.0 4.7 add_add_fusion
  731.7 64.1 %all-reduce.7.cloned.1.call-done = (f32[768,64]{0,1:T(8,128)}, f32[64,768]{1,0:T(8,128)}, f32[768,64]{0,1:T(8,128)}, f32[64,768]{1,0:T(8,128)}) async-done(((f32[768,64]{0,1:T(8,128)}, f32[64,768]{1,0:T(8,128)}, f32[768,64]{0,1:T(8,128)}, f32[64,768]{1,0:T(8,128)}), (f32[768,64]{0,1:T(8,128)}, f32[64,768]{1,0:T(8,128)}, f32[768,64]{0,1:T(8,128)}, f32[64,768]{1,0:T(8,128)})) %all-reduce.7.cloned.1.call-update) | async-done | bytes 786448 | tf_op jit(solution)/shard_map/psum | solution.py:213
  (211 shorter events, 104.1 us)
Async XLA Ops:
  7.2 247.3 %copy-start = (bf16[768,768]{1,0:T(8,128)(2,1)S(1)}, bf16[768,768]{1,0:T(8,128)(2,1)}, u32[]{:S(2)}) copy-start(bf16[768,768]{1,0:T(8,128)(2,1)} %param.27) | copy-start | bytes 3538948
  7.2 74.9 %all-gather.5.cloned.1.call-start = ((), (), s32[]{:S(2)}) async-start(), calls=%async_computation.3 | async-start | bytes 11796480 | tf_op jit(solution)/shard_map/all_gather | solution.py:141
  13.8 136.0 %all-gather.3.cloned.1.call-start = ((), (), s32[]{:S(2)}) async-start(), calls=%async_computation.2 | async-start | bytes 11796480 | tf_op jit(solution)/shard_map/all_gather | solution.py:142
  17.8 2.6 copy-start.33
  20.3 657.8 %all-reduce.9.cloned.1.call-start = ((), (), s32[]{:S(2)}) async-start(), calls=%async_computation.7 | async-start | bytes 1572864 | tf_op jit(solution)/shard_map/psum | solution.py:214
  31.6 4.6 copy-start.6
  31.6 4.6 copy-start.24
  183.3 1.3 copy-start.13
  206.0 1.3 copy-start.13
  228.6 1.3 copy-start.13
  242.4 7.0 copy-start.2
  242.4 7.0 copy-start.18
  254.5 3.9 copy-start.22
  254.5 4.8 copy-start.34
  258.4 2.9 copy-start.8
  258.4 1.0 copy-start.20
  258.4 4.6 slice-start.8
  259.4 1.9 copy-start.14
  259.4 4.1 slice-start.9
  259.4 16.2 %slice-start.6 = ((s8[4718592]{0:T(1024)(128)(4,1)}), s8[4194304]{0:T(1024)(128)(4,1)S(1)}, s32[]{:S(2)}) async-start(s8[4718592]{0:T(1024)(128)(4,1)} %bitcast.302), calls=%async_computation.14 | async-start | bytes 8388608
  261.3 64.7 %copy-start.9 = (f32[1536,768]{1,0:T(8,128)}, f32[1536,768]{1,0:T(8,128)S(1)}, u32[]{:S(2)}) copy-start(f32[1536,768]{1,0:T(8,128)S(1)} %get-tuple-element.279) | copy-start | bytes 14155780
  261.3 3.2 copy-start.32
  261.4 3.2 copy-start.36
  264.6 11.1 %slice-start.7 = ((s8[4718592]{0:T(1024)(128)(4,1)}), s8[524288]{0:T(1024)(128)(4,1)S(1)}, s32[]{:S(2)}) async-start(s8[4718592]{0:T(1024)(128)(4,1)} %bitcast.302), calls=%async_computation.15 | async-start | bytes 1048576
  275.6 49.6 %copy-start.17 = (bf16[768,64]{0,1:T(8,128)(2,1)S(1)}, bf16[768,64]{0,1:T(8,128)(2,1)}, u32[]{:S(2)}) copy-start(bf16[768,64]{0,1:T(8,128)(2,1)} %param.32) | copy-start | bytes 294916
  325.2 0.9 copy-start.19
  328.7 1.7 copy-start.7
  328.7 1.7 copy-start.25
  329.4 3.7 copy-start.26
  329.4 3.7 copy-start.29
  336.7 4.0 copy-start.4
  367.5 4.7 copy-start.15
  367.6 4.7 copy-start.21
  372.2 2.8 copy-start.5
  372.2 2.8 slice-start.2
  373.1 3.3 slice-start.3
  376.4 1.2 copy-start.23
  384.1 9.7 %copy-start.3 = (bf16[3,4,128,12,64]{2,4,3,1,0:T(8,128)(2,1)S(1)}, bf16[3,4,128,12,64]{2,4,3,1,0:T(8,128)(2,1)}, u32[]{:S(2)}) copy-start(bf16[3,4,128,12,64]{2,4,3,1,0:T(8,128)(2,1)} %copy-done.2) | copy-start | bytes 7077892
  393.7 284.4 %reduce-scatter.9.cloned.1.call-start = ((), (), s32[]{:S(2)}) async-start(), calls=%async_computation.5 | async-start | bytes 11796480
  409.4 8.2 %copy-start.10 = (bf16[3,4,128,12,64]{2,4,3,1,0:T(8,128)(2,1)S(1)}, bf16[3,4,128,12,64]{2,4,3,1,0:T(8,128)(2,1)}, u32[]{:S(2)}) copy-start(bf16[3,4,128,12,64]{2,4,3,1,0:T(8,128)(2,1)} %get-tuple-element.512) | copy-start | bytes 7077892 | tf_op jit(solution)/shard_map/while
  422.0 2.7 copy-start.11
  444.9 8.1 %copy-start.10 = (bf16[3,4,128,12,64]{2,4,3,1,0:T(8,128)(2,1)S(1)}, bf16[3,4,128,12,64]{2,4,3,1,0:T(8,128)(2,1)}, u32[]{:S(2)}) copy-start(bf16[3,4,128,12,64]{2,4,3,1,0:T(8,128)(2,1)} %get-tuple-element.512) | copy-start | bytes 7077892 | tf_op jit(solution)/shard_map/while
  457.4 2.7 copy-start.11
  480.4 8.1 %copy-start.10 = (bf16[3,4,128,12,64]{2,4,3,1,0:T(8,128)(2,1)S(1)}, bf16[3,4,128,12,64]{2,4,3,1,0:T(8,128)(2,1)}, u32[]{:S(2)}) copy-start(bf16[3,4,128,12,64]{2,4,3,1,0:T(8,128)(2,1)} %get-tuple-element.512) | copy-start | bytes 7077892 | tf_op jit(solution)/shard_map/while
  492.9 2.8 copy-start.11
  557.0 159.8 %reduce-scatter.7.cloned.1.call-start = ((), (), s32[]{:S(2)}) async-start(), calls=%async_computation.4 | async-start | bytes 11796480
  614.1 1.7 copy-start.12
  614.1 181.6 %all-reduce.7.cloned.1.call-start = ((), (), s32[]{:S(2)}) async-start(), calls=%async_computation.6 | async-start | bytes 1572864 | tf_op jit(solution)/shard_map/psum | solution.py:213
  615.7 7.3 copy-start.27
  615.8 7.3 copy-start.28
  615.8 7.3 copy-start.30
  615.8 7.3 copy-start.31
  685.6 38.8 %copy-start.35 = (bf16[768,768]{1,0:T(8,128)(2,1)S(1)}, bf16[768,768]{1,0:T(8,128)(2,1)}, u32[]{:S(2)}) copy-start(bf16[768,768]{1,0:T(8,128)(2,1)} %param.25) | copy-start | bytes 3538948
  721.6 4.9 slice-start
  721.6 4.9 slice-start.4
  724.4 2.1 slice-start.1
  724.4 2.1 slice-start.5
  724.4 2.5 copy-start.16
  727.0 75.2 %copy-start.1 = (bf16[768,768]{1,0:T(8,128)(2,1)S(1)}, bf16[768,768]{1,0:T(8,128)(2,1)}, u32[]{:S(2)}) copy-start(bf16[768,768]{1,0:T(8,128)(2,1)} %param.27) | copy-start | bytes 3538948
Sparse Core Ops, SparseCore 0:
  13.9 68.1 all-gather.4
  84.2 65.4 all-gather.2
  393.9 34.9 all-reduce.8
  557.1 78.7 reduce-scatter.8
  638.4 78.4 reduce-scatter.6
  720.4 75.2 all-reduce.6
